TPU v7x, 32 devices: a whole 2x2x4 slice. The times are simulated.
32 devices in a mesh: ctx: 8 (over z, x), head: 4 (over y, core).
Axes of the slice: x: 2, y: 2, z: 4, core: 2. Of those that a mesh axis runs over, the one named last changes fastest.
Arguments:
- qkv: bfloat16 [4096, 12288], P(('ctx', 'head')), may hold values from -26 to 26
- grad_out: bfloat16 [4096, 4096], P(('ctx', 'head')), may hold values from -6 to 6
- key_lists: int32 [32, 4], P('ctx'), may hold values from 0 to 31, as said below
- live_counts: int32 [32], P('ctx'), may hold values from 1 to 4
Outputs:
- grad_qkv: bfloat16 [4096, 12288], P(('ctx', 'head'))
Inputs may be any that keep to these rules, and one draw needn't show every extreme that they name: `key_lists`: each entry names a block whose index of ctx is within 2 of its query block's and which is not within one block of its query block; the 4 entries of a row differ. Over all 4 entries of all rows (live or not) of one index of ctx, the blocks named on any other index of ctx are at most 2 of its blocks, and this is reached.
All inputs are finite; a program needn't handle non-finite values.
Results may differ from a plain program's by a relative error of at most 0.008.
Values may be sent and summed in bfloat16 or wider, within the bound.
A program may use at most 192 MiB of HBM per device.

v0:
```python
import functools

import jax
import jax.numpy as jnp
from jax import lax
from jax.experimental import pallas as pl
from jax.experimental.pallas import tpu as pltpu
from jax.sharding import Mesh, PartitionSpec as P

HD = 128
BLK = 128
TILES = 4
LISTED = 4
NAMED = 2
PAIR = 2 * TILES
EDGE = NAMED + TILES
ALL = 2 * EDGE + PAIR
SCALE = HD ** (-0.5)
MESH = pl.DeviceIdType.MESH
TOGETHER = 2
F32 = jnp.float32
BF16 = jnp.bfloat16


def rows(block, count=1):
    start = block * BLK
    return pl.ds(start if isinstance(start, int) else pl.multiple_of(start, BLK), count * BLK)


def position(sizes):
    pairs_total, heads_total, ways = sizes
    z = lax.axis_index("cz")
    me = lax.axis_index("cx") * heads_total + lax.axis_index("head")
    return z, me


def peer_id(peer, sizes):
    return {"cx": peer // sizes[1], "head": peer % sizes[1]}


def greet(sizes):
    pairs_total, _, ways = sizes
    z, me = position(sizes)
    barrier = pltpu.get_barrier_semaphore()

    def signal(device_id):
        pl.semaphore_signal(barrier, inc=1, device_id=device_id, device_id_type=MESH)

    for k in range(1, ways):
        signal(peer_id((me + k) % ways, sizes))
    pl.when(z > 0)(lambda: signal({"cz": z - 1}))
    pl.when(z < pairs_total - 1)(lambda: signal({"cz": z + 1}))
    pl.semaphore_wait(barrier, ways - 1 + jnp.minimum(z, 1) + jnp.minimum(pairs_total - 1 - z, 1))


def remote(src, dst, send, recv, device_id):
    return pltpu.make_async_remote_copy(
        src_ref=src, dst_ref=dst, send_sem=send, recv_sem=recv, device_id=device_id, device_id_type=MESH
    )


def layer_kernel(
    sizes, slots, places, info, order, begins, qkv, grads, out,
    own, left, right, stage, pairs, acc, listed, sums, own_grads, left_grads, right_grads, from_next, from_prev, joined,
    send, recv, local, edge_send, edge_recv, back_edge_send, back_edge_recv, back_send, back_recv, back_local,
):
    pairs_total, _, ways = sizes
    heads = own.shape[0]
    z, me = position(sizes)
    wide, slim = 3 * HD, HD
    inner = (z > 0, z < pairs_total - 1)
    kv = pl.ds(HD, 2 * HD)
    greet(sizes)

    def pieces(h, device, block):
        at = device * heads + h
        return (
            (qkv.at[:, pl.ds(pl.multiple_of(at * wide, HD), wide)], own.at[h, rows(block), pl.ds(0, wide)]),
            (grads.at[:, pl.ds(pl.multiple_of(at * slim, HD), slim)], own.at[h, rows(block), pl.ds(wide, slim)]),
        )

    sends, locals_ = [], []
    for h in range(heads):
        for k in range(1, ways):
            peer = (me + k) % ways
            for t, (src, dst) in enumerate(pieces(h, peer, me)):
                copy = remote(src, dst, send.at[h, k, t], recv.at[h, k, t], peer_id(peer, sizes))
                copy.start()
                sends.append(copy)
        for t, (src, dst) in enumerate(pieces(h, me, me)):
            copy = pltpu.make_async_copy(src, dst, local.at[h, t])
            copy.start()
            locals_.append(copy)

    @pl.when(z == 0)
    def _():
        left[...] = jnp.zeros_like(left)
        from_prev[...] = jnp.zeros_like(from_prev)

    @pl.when(z == pairs_total - 1)
    def _():
        right[...] = jnp.zeros_like(right)
        from_next[...] = jnp.zeros_like(from_next)

    def edge_copies(h):
        up = [
            remote(src, left.at[h, part], edge_send.at[h, 0, n], edge_recv.at[h, 0, n], {"cz": z + 1})
            for n, (src, part) in enumerate(
                ((stage.at[h, 0], rows(0, NAMED)), (own.at[h, rows(TILES, TILES), kv], rows(NAMED, TILES)))
            )
        ]
        down = [
            remote(src, right.at[h, part], edge_send.at[h, 1, n], edge_recv.at[h, 1, n], {"cz": z - 1})
            for n, (src, part) in enumerate(
                ((stage.at[h, 1], rows(TILES, NAMED)), (own.at[h, rows(0, TILES), kv], rows(0, TILES)))
            )
        ]
        return up, down

    def back_edge_copies(h):
        up = remote(right_grads.at[h], from_prev.at[h], back_edge_send.at[h, 0], back_edge_recv.at[h, 0], {"cz": z + 1})
        down = remote(left_grads.at[h], from_next.at[h], back_edge_send.at[h, 1], back_edge_recv.at[h, 1], {"cz": z - 1})
        return [up], [down]

    def start(copies):
        up, down = copies
        pl.when(inner[1])(lambda: [c.start() for c in up] and None)
        pl.when(inner[0])(lambda: [c.start() for c in down] and None)

    def arrive(copies):
        up, down = copies
        pl.when(inner[0])(lambda: [c.wait_recv() for c in up] and None)
        pl.when(inner[1])(lambda: [c.wait_recv() for c in down] and None)

    def leave(copies):
        up, down = copies
        pl.when(inner[1])(lambda: [c.wait_send() for c in up] and None)
        pl.when(inner[0])(lambda: [c.wait_send() for c in down] and None)

    def edges(h):
        for k in range(1, ways):
            source = (me + ways - k) % ways
            for t, (src, dst) in enumerate(pieces(h, source, source)):
                remote(src, dst, send.at[h, k, t], recv.at[h, k, t], peer_id(source, sizes)).wait_recv()
        locals_[2 * h].wait()
        locals_[2 * h + 1].wait()
        for s in range(NAMED):
            for side in range(2):
                chosen = own[h, rows(side * TILES), HD : 3 * HD]
                for t in range(1, TILES):
                    chosen = jnp.where(slots[side, s] == t, own[h, rows(side * TILES + t), HD : 3 * HD], chosen)
                stage[h, side, rows(s), :] = chosen
        start(edge_copies(h))

    def attend(h):
        arrive(edge_copies(h))
        pairs[:EDGE] = left[h].reshape(EDGE, BLK, 2 * HD)
        pairs[EDGE : EDGE + PAIR] = own[h, :, HD : 3 * HD].reshape(PAIR, BLK, 2 * HD)
        pairs[EDGE + PAIR :] = right[h].reshape(EDGE, BLK, 2 * HD)
        acc[...] = jnp.zeros_like(acc)

        def step(i, carry):
            q = own[h, rows(i), :HD]
            g = own[h, rows(i), 3 * HD :]
            zero = jnp.zeros_like(q)
            both = jnp.concatenate(
                [jnp.concatenate([q, zero], axis=1), jnp.concatenate([zero, g], axis=1)], axis=0
            )
            live = info[0, i]
            usable = [info[1, i] > 0, None, info[2, i] > 0] + [live > j for j in range(LISTED)]
            kv = jnp.concatenate(
                [pairs[EDGE - 1 + i + n] for n in range(3)] + [pairs[places[i, j]] for j in range(LISTED)], axis=0
            )
            products = lax.dot_general(kv, both, (((1,), (1,)), ((), ())), preferred_element_type=F32)
            scores = []
            for n, ok in enumerate(usable):
                s = products[n * BLK : (n + 1) * BLK, :HD] * SCALE
                scores.append(s if ok is None else jnp.where(ok, s, -1e30))
            scores = jnp.concatenate(scores, axis=0)
            powers = jnp.exp(scores - jnp.max(scores, axis=0, keepdims=True))
            soft = powers * (1.0 / jnp.sum(powers, axis=0, keepdims=True))
            dp = products[:, HD:]
            ds = soft * (dp - jnp.sum(soft * dp, axis=0, keepdims=True))
            ds_low = ds.astype(BF16)
            low = jnp.concatenate([ds_low, soft.astype(BF16)], axis=1)
            terms = jnp.dot(low, both, preferred_element_type=F32)
            grad_q = lax.dot_general(ds_low, kv[:, :HD], (((0,), (0,)), ((), ())), preferred_element_type=F32)
            joined[h, rows(i), :HD] = (grad_q * SCALE).astype(BF16)
            acc[rows(EDGE - 1 + i, 3), :] += terms[: 3 * BLK]
            for j in range(LISTED):
                listed[i * LISTED + j] = terms[(3 + j) * BLK : (4 + j) * BLK]
            return carry

        lax.fori_loop(0, PAIR, step, 0)
        sums[0] = jnp.zeros((BLK, 2 * HD), F32)

        def add_up(n, carry):
            sums[n + 1] = sums[n] + listed[order[n]]
            return carry

        lax.fori_loop(0, PAIR * LISTED, add_up, 0)

        def total(p):
            value = acc[rows(p), :] + (sums[begins[p + 1]] - sums[begins[p]])
            return jnp.concatenate([value[:, :HD] * SCALE, value[:, HD:]], axis=1)

        def edge_total(p, carry):
            left_grads[h, rows(p), :] = total(p).astype(BF16)
            right_grads[h, rows(p), :] = total(EDGE + PAIR + p).astype(BF16)
            return carry

        def own_total(p, carry):
            own_grads[h, rows(p), :] = total(EDGE + p)
            return carry

        lax.fori_loop(0, EDGE, edge_total, 0)
        start(back_edge_copies(h))
        lax.fori_loop(0, PAIR, own_total, 0)

    def columns(device, h):
        return out.at[:, pl.ds(pl.multiple_of((device * heads + h) * wide, HD), wide)]

    back_sends, back_locals = [], []

    def combine(h):
        arrive(back_edge_copies(h))
        for t in range(PAIR):
            value = own_grads[h, rows(t), :]
            if t < TILES:
                near, far, table, base = from_prev, from_next, 0, t
                near_at, far_at = t, 0
            else:
                near, far, table, base = from_next, from_prev, 1, t - TILES
                near_at, far_at = NAMED + t - TILES, TILES
            value += near[h, rows(near_at), :].astype(F32)
            for s in range(NAMED):
                term = far[h, rows(far_at + s), :].astype(F32)
                value += jnp.where(slots[table, s] == base, term, 0.0)
            joined[h, rows(t), HD:] = value.astype(BF16)
        for k in range(1, ways):
            peer = (me + k) % ways
            copy = remote(
                joined.at[h, rows(peer)], columns(me, h), back_send.at[h, k], back_recv.at[h, k], peer_id(peer, sizes)
            )
            copy.start()
            back_sends.append(copy)
        copy = pltpu.make_async_copy(joined.at[h, rows(me)], columns(me, h), back_local.at[h])
        copy.start()
        back_locals.append(copy)

    for n in range(heads + 2):
        if n < heads:
            edges(n)
        if 0 <= n - 1 < heads:
            attend(n - 1)
        if 0 <= n - 2 < heads:
            combine(n - 2)

    for h in range(heads):
        for k in range(1, ways):
            source = (me + ways - k) % ways
            remote(
                joined.at[h, rows(source)], columns(source, h), back_send.at[h, k], back_recv.at[h, k],
                peer_id(source, sizes),
            ).wait_recv()
        back_locals[h].wait()
        leave(edge_copies(h))
        leave(back_edge_copies(h))
    for copy in sends + back_sends:
        copy.wait_send()


def tables(key_lists, live_counts, axes):
    pair_axis, half_axis = axes
    pairs_total = lax.axis_size(pair_axis)
    z = lax.axis_index(pair_axis)
    x = lax.axis_index(half_axis)
    mine = jnp.concatenate([key_lists, live_counts[:, None]], axis=1)
    runs = 2 * pairs_total
    steps = range(pairs_total - 1)
    other = lax.ppermute(mine, axes, [(i, i + 1 - 2 * (i % 2)) for i in range(runs)])
    straight = lax.ppermute(mine, axes, [(2 * i + 2, 2 * i) for i in steps] + [(2 * i + 1, 2 * i + 3) for i in steps])
    across = lax.ppermute(mine, axes, [(2 * i + 2, 2 * i + 1) for i in steps] + [(2 * i + 1, 2 * i + 2) for i in steps])
    after = jnp.where(x == 0, straight, across)
    before = jnp.where(x == 0, across, straight)
    pair = jnp.where(x == 0, jnp.concatenate([mine, other]), jnp.concatenate([other, mine]))
    base = z * PAIR
    lists = jnp.stack([after, before, pair[:TILES], pair[TILES:]])[:, :, :LISTED]
    lists = lists.reshape(4, TILES * LISTED)
    first = base + jnp.array([0, TILES, -PAIR, PAIR + TILES], jnp.int32)
    order = jnp.arange(TILES, dtype=jnp.int32)
    needed = jnp.any(lists[:, :, None] == (first[:, None] + order[None, :])[:, None, :], axis=1)
    earlier = order[None, :] < order[:, None]
    rank = jnp.sum(jnp.where(earlier[None] & needed[:, None, :], 1, 0), axis=2)
    slot = jnp.arange(NAMED, dtype=jnp.int32)
    chosen = needed[:, None, :] & (rank[:, None, :] == slot[None, :, None])
    slots = jnp.sum(jnp.where(chosen, order[None, None, :], 0), axis=2).astype(jnp.int32)[:2]
    rel = pair[:, :LISTED] - base
    pick = lambda table, at: jnp.sum(jnp.where(at[:, :, None] == order, table, 0), axis=2)
    far_left = pick(rank[2], rel + PAIR)
    far_right = EDGE + PAIR + TILES + pick(rank[3], rel - PAIR - TILES)
    places = jnp.where(rel < -TILES, far_left, jnp.where(rel >= PAIR + TILES, far_right, EDGE + rel))
    places = jnp.clip(places, 0, ALL - 1).astype(jnp.int32)
    block = base + jnp.arange(PAIR, dtype=jnp.int32)
    last = pairs_total * PAIR - 1
    info = jnp.stack([pair[:, LISTED], (block > 0).astype(jnp.int32), (block < last).astype(jnp.int32)])
    flat = places.reshape(-1)
    spot = jnp.arange(flat.shape[0], dtype=jnp.int32)
    ahead = (flat[None, :] < flat[:, None]) | ((flat[None, :] == flat[:, None]) & (spot[None, :] < spot[:, None]))
    at = jnp.sum(ahead.astype(jnp.int32), axis=1)
    order = jnp.sum(jnp.where(at[None, :] == spot[:, None], spot[None, :], 0), axis=1).astype(jnp.int32)
    begins = jnp.sum((flat[None, :] < jnp.arange(ALL + 1, dtype=jnp.int32)[:, None]).astype(jnp.int32), axis=1)
    return slots, places, info, order, begins.astype(jnp.int32)


def shards(qkv, grad_out, key_lists, live_counts):
    heads_total = lax.axis_size("head")
    ways = lax.axis_size("cx") * heads_total
    sizes = (lax.axis_size("cz"), heads_total, ways)
    scalars = tables(key_lists, live_counts, ("cz", "cx"))
    heads = qkv.shape[1] // (3 * HD) // ways
    full = qkv.shape[0] * ways
    smem = pl.BlockSpec(memory_space=pltpu.SMEM)
    anywhere = pl.BlockSpec(memory_space=pl.ANY)
    dma = pltpu.SemaphoreType.DMA
    edge = pltpu.VMEM((heads, EDGE * BLK, 2 * HD), BF16)
    return pl.pallas_call(
        functools.partial(layer_kernel, sizes),
        in_specs=[smem] * len(scalars) + [anywhere, anywhere],
        out_specs=anywhere,
        out_shape=jax.ShapeDtypeStruct(qkv.shape, BF16),
        scratch_shapes=[
            pltpu.VMEM((heads, full, 4 * HD), BF16), edge, edge,
            pltpu.VMEM((heads, 2, NAMED * BLK, 2 * HD), BF16),
            pltpu.VMEM((ALL, BLK, 2 * HD), BF16),
            pltpu.VMEM((ALL * BLK, 2 * HD), F32),
            pltpu.VMEM((PAIR * LISTED, BLK, 2 * HD), F32),
            pltpu.VMEM((PAIR * LISTED + 1, BLK, 2 * HD), F32),
            pltpu.VMEM((heads, full, 2 * HD), F32),
            edge, edge, edge, edge,
            pltpu.VMEM((heads, full, 3 * HD), BF16),
            dma((heads, ways, 2)), dma((heads, ways, 2)), dma((heads, 2)),
            dma((heads, 2, 2)), dma((heads, 2, 2)), dma((heads, 2)), dma((heads, 2)),
            dma((heads, ways)), dma((heads, ways)), dma((heads,)),
        ],
        compiler_params=pltpu.CompilerParams(collective_id=0, has_side_effects=True),
        name="layer",
    )(*scalars, qkv, grad_out)


def solution(mesh):
    ctx, head = mesh.shape["ctx"], mesh.shape["head"]
    split = Mesh(mesh.devices.reshape(ctx // 2, 2, head), ("cz", "cx", "head"))
    both = ("cz", "cx")
    tokens = P((*both, "head"), None)
    return jax.shard_map(
        shards, mesh=split, in_specs=(tokens, tokens, P(both, None), P(both)), out_specs=tokens, check_vma=False
    )
```

profile of v0, /device:TPU:0, one launch (start us, length us, event | category | flops | bytes accessed | tf_op | source)
XLA Modules:
  0.0 123.6 jit_solution(7028576443110296096)
XLA Ops:
  0.0 0.7 copy.8
  0.7 0.8 pad_add_fusion.3
  1.5 2.9 %collective-permute-start.2 = (s32[4,5]{1,0:T(4,128)S(1)}, s32[4,5]{1,0:T(4,128)S(1)}, u32[]{:S(2)}, u32[]{:S(2)}) collective-permute-start(s32[4,5]{1,0:T(4,128)S(1)} %pad_add_fusion.3), channel_id=1, source_target_pairs={{0,4},{4,0},{8,12},{12,8},{16,20},{20,16},{24,28},{28,24},{1,5},{5... | collective-permute-start | bytes 248 | tf_op jit(solution)/shard_map/ppermute | solution.py:281
  4.4 0.6 collective-permute-start.1
  5.1 1.3 %collective-permute-start = (s32[4,5]{1,0:T(4,128)S(1)}, s32[4,5]{1,0:T(4,128)S(1)}, u32[]{:S(2)}, u32[]{:S(2)}) collective-permute-start(s32[4,5]{1,0:T(4,128)S(1)} %pad_add_fusion.3), channel_id=1, source_target_pairs={{8,0},{16,8},{24,16},{4,12},{12,20},{20,28},{9,1},{17,9},{25,17},{... | collective-permute-start | bytes 248 | tf_op jit(solution)/shard_map/ppermute | solution.py:282
  6.4 0.7 broadcast_add_fusion
  7.1 0.1 iota_add_fusion
  7.2 0.0 collective-permute-done.2
  7.2 0.8 add_select_fusion
  8.0 0.2 slice_reduce_fusion
  8.2 0.0 collective-permute-done.1
  8.2 3.2 %collective-permute-done = s32[4,5]{1,0:T(4,128)S(1)} collective-permute-done((s32[4,5]{1,0:T(4,128)S(1)}, s32[4,5]{1,0:T(4,128)S(1)}, u32[]{:S(2)}, u32[]{:S(2)}) %collective-permute-start) | collective-permute-done | bytes 112 | tf_op jit(solution)/shard_map/ppermute | solution.py:282
  11.4 0.1 eq.35
  11.5 0.2 compare_reduce_fusion
  11.7 0.2 select_reduce_fusion.3
  11.9 0.1 select_reduce_fusion.4
  12.0 0.1 copy.11
  12.1 0.1 copy.10
  12.2 0.1 select_reduce_fusion.1
  12.3 0.1 copy.12
  12.4 0.1 copy.13
  12.5 0.0 copy-start
  12.5 0.1 lt.81
  12.5 0.6 convert_reduce_fusion.1.begins
  13.2 0.2 convert_reduce_fusion
  13.4 0.6 copy.14.slots
  14.0 0.7 select_reduce_fusion.order
  14.7 0.6 pad_add_fusion.4.info
  15.3 0.0 copy-done
  15.3 104.4 %layer.1 = bf16[128,12288]{1,0:T(8,128)(2,1)} custom-call(s32[2,2]{1,0:T(2,128)} %copy.14.slots, s32[8,4]{1,0:T(8,128)} %copy-done, s32[3,8]{1,0:T(4,128)} %pad_add_fusion.4.info, s32[32]{0:T(128)} %select_reduce_fusion.order, s32[21]{0:T(128)} %convert_reduce_fusion.1.begins, bf16[128,12288]{1,0:T(8,128)(2,1)} %qkv.1, bf16[128,4096]{1,0:T(8,128)(2,1)} %grads.1), custom_call_target="tpu_custom_call" | custom-call | tf_op jit(solution)/shard_map/layer/pallas_call | solution.py:327
  119.7 3.8 %copy.16 = bf16[128,12288]{1,0:T(8,128)(2,1)} copy(bf16[128,12288]{1,0:T(8,128)(2,1)} %layer.1) | data formatting | bytes 6291456
  (8 shorter events, 0.0 us)
Async XLA Ops:
  1.5 5.7 %collective-permute-start.2 = (s32[4,5]{1,0:T(4,128)S(1)}, s32[4,5]{1,0:T(4,128)S(1)}, u32[]{:S(2)}, u32[]{:S(2)}) collective-permute-start(s32[4,5]{1,0:T(4,128)S(1)} %pad_add_fusion.3), channel_id=1, source_target_pairs={{0,4},{4,0},{8,12},{12,8},{16,20},{20,16},{24,28},{28,24},{1,5},{5... | collective-permute-start | bytes 248 | tf_op jit(solution)/shard_map/ppermute | solution.py:281
  4.4 3.8 %collective-permute-start.1 = (s32[4,5]{1,0:T(4,128)S(1)}, s32[4,5]{1,0:T(4,128)S(1)}, u32[]{:S(2)}, u32[]{:S(2)}) collective-permute-start(s32[4,5]{1,0:T(4,128)S(1)} %pad_add_fusion.3), channel_id=1, source_target_pairs={{8,4},{16,12},{24,20},{4,8},{12,16},{20,24},{9,5},{17,13},{25,21},... | collective-permute-start | bytes 248 | tf_op jit(solution)/shard_map/ppermute | solution.py:283
  5.1 6.3 %collective-permute-start = (s32[4,5]{1,0:T(4,128)S(1)}, s32[4,5]{1,0:T(4,128)S(1)}, u32[]{:S(2)}, u32[]{:S(2)}) collective-permute-start(s32[4,5]{1,0:T(4,128)S(1)} %pad_add_fusion.3), channel_id=1, source_target_pairs={{8,0},{16,8},{24,16},{4,12},{12,20},{20,28},{9,1},{17,9},{25,17},{... | collective-permute-start | bytes 248 | tf_op jit(solution)/shard_map/ppermute | solution.py:282
  12.5 2.8 %copy-start = (s32[8,4]{1,0:T(8,128)}, s32[8,4]{1,0:T(8,128)S(1)}, u32[]{:S(2)}) copy-start(s32[8,4]{1,0:T(8,128)S(1)} %select_clamp_fusion.places) | copy-start | bytes 388
where the time goes:
time: 125 us; the launch traced here: 124 us
  Pallas kernels  104 us (83%)
  local copies, waits for them, and re-layouts  5.88 us (5%)
  other arithmetic  5.09 us (4%)
  starting transfers between devices  4.88 us (4%)
  waiting for transfers between devices  3.2 us (3%)
    pallas_call x1, Pallas kernels, shards(): pl.pallas_call(functools.partial(layer_kernel, sizes), in_specs=[smem] *...  104 us
    unnamed x4, local copies, waits for them, and re-layouts  4.46 us
    ppermute x1, waiting for transfers between devices, tables(): lax.ppermute(mine, axes, [(2 * i + 2, 2 * i) for i in steps] + [(2 * i +...  3.19 us
    ppermute x1, starting transfers between devices, tables(): lax.ppermute(mine, axes, [(i, i + 1 - 2 * (i % 2)) for i in range(runs)])  2.94 us
  transfers between devices with their start and end apart: 3, of which 1 were waited for; matrix products, arithmetic and copies ran while one was open for 1% of the time, Pallas kernels for 0%

commit v1 on v0

v1 whole, which is shorter than its diff:
```python
import functools

import jax
import jax.numpy as jnp
from jax import lax
from jax.experimental import pallas as pl
from jax.experimental.pallas import tpu as pltpu
from jax.sharding import Mesh, PartitionSpec as P

HD = 128
BLK = 128
TILES = 4
LISTED = 4
NAMED = 2
PAIR = 2 * TILES
EDGE = NAMED + TILES
ALL = 2 * EDGE + PAIR
SCALE = HD ** (-0.5)
MESH = pl.DeviceIdType.MESH
I32 = jnp.int32
F32 = jnp.float32
BF16 = jnp.bfloat16


def rows(block, count=1):
    start = block * BLK
    return pl.ds(start if isinstance(start, int) else pl.multiple_of(start, BLK), count * BLK)


def position(sizes):
    pairs_total, heads_total, ways = sizes
    z = lax.axis_index("cz")
    me = lax.axis_index("cx") * heads_total + lax.axis_index("head")
    return z, me


def peer_id(peer, sizes):
    return {"cx": peer // sizes[1], "head": peer % sizes[1]}


def greet(sizes):
    pairs_total, _, ways = sizes
    z, me = position(sizes)
    x = lax.axis_index("cx")
    side = z - 1 + 2 * x
    inside = (side >= 0) & (side < pairs_total)
    barrier = pltpu.get_barrier_semaphore()

    def signal(device_id):
        pl.semaphore_signal(barrier, inc=1, device_id=device_id, device_id_type=MESH)

    for k in range(1, ways):
        signal(peer_id((me + k) % ways, sizes))
    pl.when(z > 0)(lambda: signal({"cz": z - 1}))
    pl.when(z < pairs_total - 1)(lambda: signal({"cz": z + 1}))
    pl.when(inside)(lambda: signal({"cz": side, "cx": 1 - x}))
    neighbours = jnp.minimum(z, 1) + jnp.minimum(pairs_total - 1 - z, 1) + jnp.where(inside, 1, 0)
    pl.semaphore_wait(barrier, ways - 1 + neighbours)


def remote(src, dst, send, recv, device_id):
    return pltpu.make_async_remote_copy(
        src_ref=src, dst_ref=dst, send_sem=send, recv_sem=recv, device_id=device_id, device_id_type=MESH
    )


def pack(lists, key_lists, live_counts, pairs_total, z, x):
    row = lax.broadcasted_iota(I32, (8, 128), 0)
    col = lax.broadcasted_iota(I32, (8, 128), 1)
    value = jnp.full((8, 128), -1, I32)
    for b in range(TILES):
        for j in range(LISTED):
            value = jnp.where((row == b) & (col == j), key_lists[b, j], value)
        value = jnp.where((row == b) & (col == LISTED), live_counts[b], value)
    lists[x] = value

    @pl.when(z == pairs_total - 1)
    def _():
        lists[2] = jnp.full((8, 128), -1, I32)

    @pl.when(z == 0)
    def _():
        lists[3] = jnp.full((8, 128), -1, I32)


def tables(tab, places, slots, chains, z):
    base = z * PAIR

    def named(run, first):
        flags = [jnp.int32(0)] * TILES
        for b in range(TILES):
            for j in range(LISTED):
                at = tab[run, b, j] - first
                flags = [jnp.where(at == t, 1, flag) for t, flag in enumerate(flags)]
        ranks = [jnp.int32(0)]
        for flag in flags[:-1]:
            ranks.append(ranks[-1] + flag)
        return flags, ranks

    for side, (run, first) in enumerate(((2, base), (3, base + TILES))):
        flags, ranks = named(run, first)
        for s in range(NAMED):
            chosen = jnp.int32(0)
            for t in range(TILES):
                chosen = jnp.where((flags[t] == 1) & (ranks[t] == s), t, chosen)
            slots[side, s] = chosen
    row = lax.broadcasted_iota(I32, (8, 128), 0)
    col = lax.broadcasted_iota(I32, (8, 128), 1)
    before = jnp.zeros((8, 128), I32)
    last = jnp.zeros((8, 128), I32)
    along = jnp.full((8, 128), -1, I32)
    found = []
    for run, (first, start) in enumerate(((base - PAIR, 0), (base + PAIR + TILES, EDGE + PAIR + TILES))):
        _, ranks = named(run, first)
        for b in range(TILES):
            for j in range(LISTED):
                block = tab[run, b, j]
                far = jnp.int32(0)
                for t in range(1, TILES):
                    far = jnp.where(block - first == t, ranks[t], far)
                outside = (block < base - TILES) if run == 0 else (block >= base + PAIR + TILES)
                place = jnp.where(outside, start + far, EDGE + block - base)
                place = jnp.clip(place, 0, ALL - 1)
                places[run * TILES + b, j] = place
                found.append(place)
    for n, place in enumerate(found):
        along = jnp.where(col == n, place, along)
    for n, place in enumerate(found):
        before = jnp.where((along == place) & (col > n), n + 1, before)
        last = jnp.where(col == place, n + 1, last)
    chains[...] = jnp.where(row == 0, before, last)


def layer_kernel(
    sizes, key_lists, live_counts, qkv, grads, out,
    own, left, right, stage, pairs, acc, chain, own_grads, left_grads, right_grads, from_next, from_prev, joined,
    lists, chains, tab, links, places, slots,
    send, recv, local, edge_send, edge_recv, back_edge_send, back_edge_recv, back_send, back_recv, back_local,
    list_send, list_recv, table_sem,
):
    pairs_total, _, ways = sizes
    heads = own.shape[0]
    z, me = position(sizes)
    x = lax.axis_index("cx")
    wide, slim = 3 * HD, HD
    inner = (z > 0, z < pairs_total - 1)
    kv = pl.ds(HD, 2 * HD)
    pack(lists, key_lists, live_counts, pairs_total, z, x)
    greet(sizes)

    def piece(h, device, block, t):
        at = device * heads + h
        start = pl.multiple_of(at * wide, HD)
        if t == 0:
            return qkv.at[:, pl.ds(start + HD, 2 * HD)], own.at[h, rows(block), kv]
        if t == 1:
            return qkv.at[:, pl.ds(start, HD)], own.at[h, rows(block), pl.ds(0, HD)]
        return grads.at[:, pl.ds(pl.multiple_of(at * slim, HD), slim)], own.at[h, rows(block), pl.ds(wide, slim)]

    side = z - 1 + 2 * x
    beyond = (side >= 0) & (side < pairs_total)
    list_other = remote(lists.at[x], lists.at[x], list_send.at[0], list_recv.at[0], {"cx": 1 - x})
    list_side = [
        remote(lists.at[x], lists.at[2 + x], list_send.at[1], list_recv.at[1 + x], {"cz": side}),
        remote(lists.at[x], lists.at[2 + x], list_send.at[2], list_recv.at[1 + x], {"cz": side, "cx": 1 - x}),
    ]
    list_other.start()
    pl.when(beyond)(lambda: [c.start() for c in list_side] and None)

    sends = []

    def fetch(h, kinds):
        for k in range(1, ways):
            peer = (me + k) % ways
            for t in kinds:
                src, dst = piece(h, peer, me, t)
                copy = remote(src, dst, send.at[h, k, t], recv.at[h, k, t], peer_id(peer, sizes))
                copy.start()
                sends.append(copy)
        for t in kinds:
            src, dst = piece(h, me, me, t)
            pltpu.make_async_copy(src, dst, local.at[h, t]).start()

    def arrived(h, kinds):
        for t in kinds:
            for k in range(1, ways):
                source = (me + ways - k) % ways
                src, dst = piece(h, source, source, t)
                remote(src, dst, send.at[h, k, t], recv.at[h, k, t], peer_id(source, sizes)).wait_recv()
            src, dst = piece(h, me, me, t)
            pltpu.make_async_copy(src, dst, local.at[h, t]).wait()

    ahead = [("kv", 0), ("rest", 0), ("kv", 1)]
    for h in range(2, heads):
        ahead += [("kv", h), ("rest", h - 1)]
    ahead += [("rest", heads - 1)] if heads > 1 else []
    for kind, h in ahead:
        if h < heads:
            fetch(h, (0,) if kind == "kv" else (1, 2))

    @pl.when(z == 0)
    def _():
        left[...] = jnp.zeros_like(left)
        from_prev[...] = jnp.zeros_like(from_prev)

    @pl.when(z == pairs_total - 1)
    def _():
        right[...] = jnp.zeros_like(right)
        from_next[...] = jnp.zeros_like(from_next)

    chain[0] = jnp.zeros((BLK, 2 * HD), F32)

    list_other_in = remote(lists.at[1 - x], lists.at[1 - x], list_send.at[0], list_recv.at[0], {"cx": 1 - x})
    list_other_in.wait_recv()
    for n, there in ((0, inner[1]), (1, inner[0])):
        come = remote(lists.at[2 + n], lists.at[2 + n], list_send.at[1], list_recv.at[1 + n], {"cx": 1 - x})
        pl.when(there)(come.wait_recv)
    copy = pltpu.make_async_copy(lists, tab, table_sem.at[0])
    copy.start()
    copy.wait()
    tables(tab, places, slots, chains, z)
    copy = pltpu.make_async_copy(chains, links, table_sem.at[1])
    copy.start()
    copy.wait()

    def edge_copies(h):
        up = [
            remote(src, left.at[h, part], edge_send.at[h, 0, n], edge_recv.at[h, 0, n], {"cz": z + 1})
            for n, (src, part) in enumerate(
                ((stage.at[h, 0], rows(0, NAMED)), (own.at[h, rows(TILES, TILES), kv], rows(NAMED, TILES)))
            )
        ]
        down = [
            remote(src, right.at[h, part], edge_send.at[h, 1, n], edge_recv.at[h, 1, n], {"cz": z - 1})
            for n, (src, part) in enumerate(
                ((stage.at[h, 1], rows(TILES, NAMED)), (own.at[h, rows(0, TILES), kv], rows(0, TILES)))
            )
        ]
        return up, down

    def back_edge_copies(h):
        up = remote(right_grads.at[h], from_prev.at[h], back_edge_send.at[h, 0], back_edge_recv.at[h, 0], {"cz": z + 1})
        down = remote(left_grads.at[h], from_next.at[h], back_edge_send.at[h, 1], back_edge_recv.at[h, 1], {"cz": z - 1})
        return [up], [down]

    def start(copies):
        up, down = copies
        pl.when(inner[1])(lambda: [c.start() for c in up] and None)
        pl.when(inner[0])(lambda: [c.start() for c in down] and None)

    def arrive(copies):
        up, down = copies
        pl.when(inner[0])(lambda: [c.wait_recv() for c in up] and None)
        pl.when(inner[1])(lambda: [c.wait_recv() for c in down] and None)

    def leave(copies):
        up, down = copies
        pl.when(inner[1])(lambda: [c.wait_send() for c in up] and None)
        pl.when(inner[0])(lambda: [c.wait_send() for c in down] and None)

    def edges(h):
        arrived(h, (0,))
        for s in range(NAMED):
            for side in range(2):
                chosen = own[h, rows(side * TILES), HD : 3 * HD]
                for t in range(1, TILES):
                    chosen = jnp.where(slots[side, s] == t, own[h, rows(side * TILES + t), HD : 3 * HD], chosen)
                stage[h, side, rows(s), :] = chosen
        start(edge_copies(h))

    def attend(h, middle):
        arrived(h, (1, 2))
        arrive(edge_copies(h))
        pairs[:EDGE] = left[h].reshape(EDGE, BLK, 2 * HD)
        pairs[EDGE : EDGE + PAIR] = own[h, :, HD : 3 * HD].reshape(PAIR, BLK, 2 * HD)
        pairs[EDGE + PAIR :] = right[h].reshape(EDGE, BLK, 2 * HD)
        acc[...] = jnp.zeros_like(acc)

        def step(i, carry):
            q = own[h, rows(i), :HD]
            g = own[h, rows(i), 3 * HD :]
            zero = jnp.zeros_like(q)
            both = jnp.concatenate(
                [jnp.concatenate([q, zero], axis=1), jnp.concatenate([zero, g], axis=1)], axis=0
            )
            block = z * PAIR + i
            live = tab[i // TILES, i % TILES, LISTED]
            usable = [block > 0, None, block < pairs_total * PAIR - 1] + [live > j for j in range(LISTED)]
            kv = jnp.concatenate(
                [pairs[EDGE - 1 + i + n] for n in range(3)] + [pairs[places[i, j]] for j in range(LISTED)], axis=0
            )
            products = lax.dot_general(kv, both, (((1,), (1,)), ((), ())), preferred_element_type=F32)
            scores = []
            for n, ok in enumerate(usable):
                s = products[n * BLK : (n + 1) * BLK, :HD] * SCALE
                scores.append(s if ok is None else jnp.where(ok, s, -1e30))
            scores = jnp.concatenate(scores, axis=0)
            powers = jnp.exp(scores - jnp.max(scores, axis=0, keepdims=True))
            soft = powers * (1.0 / jnp.sum(powers, axis=0, keepdims=True))
            dp = products[:, HD:]
            ds = soft * (dp - jnp.sum(soft * dp, axis=0, keepdims=True))
            ds_low = ds.astype(BF16)
            low = jnp.concatenate([ds_low, soft.astype(BF16)], axis=1)
            terms = jnp.dot(low, both, preferred_element_type=F32)
            grad_q = lax.dot_general(ds_low, kv[:, :HD], (((0,), (0,)), ((), ())), preferred_element_type=F32)
            joined[h, rows(i), :HD] = (grad_q * SCALE).astype(BF16)
            acc[rows(EDGE - 1 + i, 3), :] += terms[: 3 * BLK]
            for j in range(LISTED):
                n = i * LISTED + j
                chain[n + 1] = terms[(3 + j) * BLK : (4 + j) * BLK] + chain[links[0, n]]
            return carry

        lax.fori_loop(0, PAIR // 2, step, 0)
        middle()
        lax.fori_loop(PAIR // 2, PAIR, step, 0)

        def total(p):
            value = acc[rows(p), :] + chain[links[1, p]]
            return jnp.concatenate([value[:, :HD] * SCALE, value[:, HD:]], axis=1)

        def edge_total(p, carry):
            left_grads[h, rows(p), :] = total(p).astype(BF16)
            right_grads[h, rows(p), :] = total(EDGE + PAIR + p).astype(BF16)
            return carry

        def own_total(p, carry):
            own_grads[h, rows(p), :] = total(EDGE + p)
            return carry

        lax.fori_loop(0, EDGE, edge_total, 0)
        start(back_edge_copies(h))
        lax.fori_loop(0, PAIR, own_total, 0)

    back_sends, back_locals = [], []
    parts = (slice(0, HD), slice(HD, 3 * HD))

    def column(device, h, t):
        first = pl.multiple_of((device * heads + h) * wide, HD)
        return out.at[:, pl.ds(first, HD)] if t == 0 else out.at[:, pl.ds(first + HD, 2 * HD)]

    def give(h, t):
        for k in range(1, ways):
            peer = (me + k) % ways
            copy = remote(
                joined.at[h, rows(peer), parts[t]], column(me, h, t), back_send.at[h, k, t], back_recv.at[h, k, t],
                peer_id(peer, sizes),
            )
            copy.start()
            back_sends.append(copy)
        copy = pltpu.make_async_copy(joined.at[h, rows(me), parts[t]], column(me, h, t), back_local.at[h, t])
        copy.start()
        back_locals.append(copy)

    def combine(h):
        arrive(back_edge_copies(h))
        for t in range(PAIR):
            value = own_grads[h, rows(t), :]
            if t < TILES:
                near, far, table, base = from_prev, from_next, 0, t
                near_at, far_at = t, 0
            else:
                near, far, table, base = from_next, from_prev, 1, t - TILES
                near_at, far_at = NAMED + t - TILES, TILES
            value += near[h, rows(near_at), :].astype(F32)
            for s in range(NAMED):
                term = far[h, rows(far_at + s), :].astype(F32)
                value += jnp.where(slots[table, s] == base, term, 0.0)
            joined[h, rows(t), HD:] = value.astype(BF16)
        give(h, 1)

    edges(0)
    for h in range(heads):
        attend(h, functools.partial(edges, h + 1) if h + 1 < heads else lambda: None)
        give(h, 0)
        if h > 0:
            combine(h - 1)
    combine(heads - 1)

    for h in range(heads):
        for t in range(2):
            for k in range(1, ways):
                source = (me + ways - k) % ways
                remote(
                    joined.at[h, rows(source), parts[t]], column(source, h, t), back_send.at[h, k, t],
                    back_recv.at[h, k, t], peer_id(source, sizes),
                ).wait_recv()
        leave(edge_copies(h))
        leave(back_edge_copies(h))
    for copy in back_locals:
        copy.wait()
    for copy in sends + back_sends:
        copy.wait_send()
    list_other.wait_send()
    pl.when(beyond)(lambda: [c.wait_send() for c in list_side] and None)


def shards(qkv, grad_out, key_lists, live_counts):
    heads_total = lax.axis_size("head")
    ways = lax.axis_size("cx") * heads_total
    sizes = (lax.axis_size("cz"), heads_total, ways)
    heads = qkv.shape[1] // (3 * HD) // ways
    full = qkv.shape[0] * ways
    smem = pl.BlockSpec(memory_space=pltpu.SMEM)
    hbm = pl.BlockSpec(memory_space=pltpu.HBM)
    dma = pltpu.SemaphoreType.DMA
    edge = pltpu.VMEM((heads, EDGE * BLK, 2 * HD), BF16)
    return pl.pallas_call(
        functools.partial(layer_kernel, sizes),
        in_specs=[smem, smem, hbm, hbm],
        out_specs=pl.BlockSpec(memory_space=pltpu.VMEM),
        out_shape=pltpu.VMEM(qkv.shape, BF16),
        scratch_shapes=[
            pltpu.VMEM((heads, full, 4 * HD), BF16), edge, edge,
            pltpu.VMEM((heads, 2, NAMED * BLK, 2 * HD), BF16),
            pltpu.VMEM((ALL, BLK, 2 * HD), BF16),
            pltpu.VMEM((ALL * BLK, 2 * HD), F32),
            pltpu.VMEM((PAIR * LISTED + 1, BLK, 2 * HD), F32),
            pltpu.VMEM((heads, full, 2 * HD), F32),
            edge, edge, edge, edge,
            pltpu.VMEM((heads, full, 3 * HD), BF16),
            pltpu.VMEM((4, 8, 128), I32), pltpu.VMEM((8, 128), I32),
            pltpu.SMEM((4, 8, 128), I32), pltpu.SMEM((8, 128), I32),
            pltpu.SMEM((PAIR, LISTED), I32), pltpu.SMEM((2, NAMED), I32),
            dma((heads, ways, 3)), dma((heads, ways, 3)), dma((heads, 3)),
            dma((heads, 2, 2)), dma((heads, 2, 2)), dma((heads, 2)), dma((heads, 2)),
            dma((heads, ways, 2)), dma((heads, ways, 2)), dma((heads, 2)),
            dma((3,)), dma((3,)), dma((2,)),
        ],
        compiler_params=pltpu.CompilerParams(
            collective_id=0, has_side_effects=True, vmem_limit_bytes=60_000_000
        ),
        name="layer",
    )(key_lists, live_counts, qkv, grad_out)


def solution(mesh):
    ctx, head = mesh.shape["ctx"], mesh.shape["head"]
    split = Mesh(mesh.devices.reshape(ctx // 2, 2, head), ("cz", "cx", "head"))
    both = ("cz", "cx")
    tokens = P((*both, "head"), None)
    return jax.shard_map(
        shards, mesh=split, in_specs=(tokens, tokens, P(both, None), P(both)), out_specs=tokens, check_vma=False
    )
```

time: 125 us -> 106 us (0.85)
  other arithmetic: 5.09 us -> 0 us
  starting transfers between devices: 4.88 us -> 0 us
  local copies, waits for them, and re-layouts: 5.88 us -> 1.67 us
  waiting for transfers between devices: 3.2 us -> 0 us
    ppermute x3 -> x0, starting transfers between devices: 4.88 us -> none  [the longest x1 2.94 us: tables(): lax.ppermute(mine, axes, [(i, i + 1 - 2 * (i % 2)) for i in range(runs)])]
    ppermute x3 -> x0, waiting for transfers between devices: 3.2 us -> none  [the longest x1 3.19 us: tables(): lax.ppermute(mine, axes, [(2 * i + 2, 2 * i) for i in steps] + [(2 * i +...]
    unnamed x4 -> x1, local copies, waits for them, and re-layouts: 4.46 us -> 1.67 us
    reduce_sum x6 -> x0, other arithmetic: 1.93 us -> none  [the longest x1 0.71 us: tables(): jnp.sum(jnp.where(at[None, :] == spot[:, None], spot[None, :], 0), axis=1)]
  transfers between devices with their start and end apart: 3 -> 0, of which waited for: 1 -> 0; matrix products, arithmetic and copies ran while one was open for 1% -> 0% of each run, Pallas kernels for 0% -> 0%
where the time goes in v1:
time: 106 us
  Pallas kernels  104 us (98%)
  local copies, waits for them, and re-layouts  1.67 us (2%)
    pallas_call x1, Pallas kernels, shards(): pl.pallas_call(functools.partial(layer_kernel, sizes), in_specs=[smem, sm...  104 us

profile of v1, /device:TPU:0, one launch (start us, length us, event | category | flops | bytes accessed | tf_op | source)
XLA Modules:
  0.0 105.5 jit_solution(10149998435200682197)
XLA Ops:
  0.0 103.8 %layer.1 = bf16[128,12288]{1,0:T(8,128)(2,1)S(1)} custom-call(s32[4,4]{1,0:T(4,128)} %key_lists.1, s32[4]{0:T(128)} %live_counts.1, bf16[128,12288]{1,0:T(8,128)(2,1)} %qkv.1, bf16[128,4096]{1,0:T(8,128)(2,1)} %grads.1), custom_call_target="tpu_custom_call" | custom-call | tf_op jit(solution)/shard_map/layer/pallas_call | solution.py:407
  103.8 1.7 %copy.6 = bf16[128,12288]{1,0:T(8,128)(2,1)} copy(bf16[128,12288]{1,0:T(8,128)(2,1)S(1)} %layer.1) | data formatting | bytes 6291456

commit v2 on v1

--- a/solution.py
+++ b/solution.py
@@ -15,7 +15,11 @@
 PAIR = 2 * TILES
 EDGE = NAMED + TILES
 ALL = 2 * EDGE + PAIR
+WIDTH = 3 + LISTED
+AHEAD = 1
+MIDDLE = 4
 SCALE = HD ** (-0.5)
+RATE = SCALE * 1.4426950408889634
 MESH = pl.DeviceIdType.MESH
 I32 = jnp.int32
 F32 = jnp.float32
@@ -133,7 +137,7 @@
 
 def layer_kernel(
     sizes, key_lists, live_counts, qkv, grads, out,
-    own, left, right, stage, pairs, acc, chain, own_grads, left_grads, right_grads, from_next, from_prev, joined,
+    own, left, right, stage, pairs, acc, chain, even, odd, own_grads, left_grads, right_grads, from_next, from_prev, joined,
     lists, chains, tab, links, places, slots,
     send, recv, local, edge_send, edge_recv, back_edge_send, back_edge_recv, back_send, back_recv, back_local,
     list_send, list_recv, table_sem,
@@ -190,13 +194,11 @@
             src, dst = piece(h, me, me, t)
             pltpu.make_async_copy(src, dst, local.at[h, t]).wait()
 
-    ahead = [("kv", 0), ("rest", 0), ("kv", 1)]
-    for h in range(2, heads):
-        ahead += [("kv", h), ("rest", h - 1)]
-    ahead += [("rest", heads - 1)] if heads > 1 else []
-    for kind, h in ahead:
+    for h in range(heads + AHEAD):
         if h < heads:
-            fetch(h, (0,) if kind == "kv" else (1, 2))
+            fetch(h, (0,))
+        if h >= AHEAD:
+            fetch(h - AHEAD, (1, 2))
 
     @pl.when(z == 0)
     def _():
@@ -238,9 +240,16 @@
         ]
         return up, down
 
-    def back_edge_copies(h):
-        up = remote(right_grads.at[h], from_prev.at[h], back_edge_send.at[h, 0], back_edge_recv.at[h, 0], {"cz": z + 1})
-        down = remote(left_grads.at[h], from_next.at[h], back_edge_send.at[h, 1], back_edge_recv.at[h, 1], {"cz": z - 1})
+    def back_edge_copies(h, t):
+        part = pl.ds(t * HD, HD)
+        up = remote(
+            right_grads.at[h, :, part], from_prev.at[h, :, part],
+            back_edge_send.at[h, 0, t], back_edge_recv.at[h, 0, t], {"cz": z + 1},
+        )
+        down = remote(
+            left_grads.at[h, :, part], from_next.at[h, :, part],
+            back_edge_send.at[h, 1, t], back_edge_recv.at[h, 1, t], {"cz": z - 1},
+        )
         return [up], [down]
 
     def start(copies):
@@ -268,7 +277,7 @@
                 stage[h, side, rows(s), :] = chosen
         start(edge_copies(h))
 
-    def attend(h, middle):
+    def attend(h, middle=None):
         arrived(h, (1, 2))
         arrive(edge_copies(h))
         pairs[:EDGE] = left[h].reshape(EDGE, BLK, 2 * HD)
@@ -276,43 +285,64 @@
         pairs[EDGE + PAIR :] = right[h].reshape(EDGE, BLK, 2 * HD)
         acc[...] = jnp.zeros_like(acc)
 
-        def step(i, carry):
+        def operand(i):
             q = own[h, rows(i), :HD]
             g = own[h, rows(i), 3 * HD :]
             zero = jnp.zeros_like(q)
-            both = jnp.concatenate(
+            return jnp.concatenate(
                 [jnp.concatenate([q, zero], axis=1), jnp.concatenate([zero, g], axis=1)], axis=0
             )
+
+        def keys(i, columns):
+            near = [pairs[EDGE - 1 + i + n, :, columns] for n in range(3)]
+            return jnp.concatenate(near + [pairs[places[i, j], :, columns] for j in range(LISTED)], axis=0)
+
+        def issue(i, slot):
+            slot[...] = lax.dot_general(
+                keys(i, slice(None)), operand(i), (((1,), (1,)), ((), ())), preferred_element_type=F32
+            )
+
+        def settle(i, products):
             block = z * PAIR + i
             live = tab[i // TILES, i % TILES, LISTED]
             usable = [block > 0, None, block < pairs_total * PAIR - 1] + [live > j for j in range(LISTED)]
-            kv = jnp.concatenate(
-                [pairs[EDGE - 1 + i + n] for n in range(3)] + [pairs[places[i, j]] for j in range(LISTED)], axis=0
-            )
-            products = lax.dot_general(kv, both, (((1,), (1,)), ((), ())), preferred_element_type=F32)
-            scores = []
-            for n, ok in enumerate(usable):
-                s = products[n * BLK : (n + 1) * BLK, :HD] * SCALE
-                scores.append(s if ok is None else jnp.where(ok, s, -1e30))
-            scores = jnp.concatenate(scores, axis=0)
-            powers = jnp.exp(scores - jnp.max(scores, axis=0, keepdims=True))
-            soft = powers * (1.0 / jnp.sum(powers, axis=0, keepdims=True))
+            tiles = [products[n * BLK : (n + 1) * BLK, :HD] for n in range(WIDTH)]
+            peaks = [jnp.max(s.reshape(BLK // 8, 8, HD), axis=0) for s in tiles]
+            peaks = [s if ok is None else jnp.where(ok, s, -1e30) for s, ok in zip(peaks, usable)]
+            shift = jnp.max(functools.reduce(jnp.maximum, peaks), axis=0, keepdims=True) * -RATE
+            shifts = [shift if ok is None else jnp.where(ok, shift, -1e30) for ok in usable]
+            powers = jnp.concatenate([jnp.exp2(s * RATE + b) for s, b in zip(tiles, shifts)], axis=0)
             dp = products[:, HD:]
-            ds = soft * (dp - jnp.sum(soft * dp, axis=0, keepdims=True))
+            over = 1.0 / jnp.sum(powers, axis=0, keepdims=True)
+            soft = powers * over
+            ds = soft * (dp - jnp.sum(powers * dp, axis=0, keepdims=True) * over)
             ds_low = ds.astype(BF16)
             low = jnp.concatenate([ds_low, soft.astype(BF16)], axis=1)
-            terms = jnp.dot(low, both, preferred_element_type=F32)
-            grad_q = lax.dot_general(ds_low, kv[:, :HD], (((0,), (0,)), ((), ())), preferred_element_type=F32)
+            terms = jnp.dot(low, operand(i), preferred_element_type=F32)
+            grad_q = lax.dot_general(
+                ds_low, keys(i, slice(0, HD)), (((0,), (0,)), ((), ())), preferred_element_type=F32
+            )
             joined[h, rows(i), :HD] = (grad_q * SCALE).astype(BF16)
             acc[rows(EDGE - 1 + i, 3), :] += terms[: 3 * BLK]
             for j in range(LISTED):
                 n = i * LISTED + j
                 chain[n + 1] = terms[(3 + j) * BLK : (4 + j) * BLK] + chain[links[0, n]]
+
+        def step(n, carry):
+            i = 2 * n
+            issue(i + 1, odd)
+            settle(i, even)
+            issue((i + 2) % PAIR, even)
+            settle(i + 1, odd)
             return carry
 
-        lax.fori_loop(0, PAIR // 2, step, 0)
-        middle()
-        lax.fori_loop(PAIR // 2, PAIR, step, 0)
+        issue(0, even)
+        if middle is None:
+            lax.fori_loop(0, PAIR // 2, step, 0)
+        else:
+            lax.fori_loop(0, MIDDLE // 2, step, 0)
+            middle()
+            lax.fori_loop(MIDDLE // 2, PAIR // 2, step, 0)
 
         def total(p):
             value = acc[rows(p), :] + chain[links[1, p]]
@@ -328,15 +358,15 @@
             return carry
 
         lax.fori_loop(0, EDGE, edge_total, 0)
-        start(back_edge_copies(h))
+        start(back_edge_copies(h, 0))
+        start(back_edge_copies(h, 1))
         lax.fori_loop(0, PAIR, own_total, 0)
 
     back_sends, back_locals = [], []
-    parts = (slice(0, HD), slice(HD, 3 * HD))
+    parts = [slice(t * HD, (t + 1) * HD) for t in range(3)]
 
     def column(device, h, t):
-        first = pl.multiple_of((device * heads + h) * wide, HD)
-        return out.at[:, pl.ds(first, HD)] if t == 0 else out.at[:, pl.ds(first + HD, 2 * HD)]
+        return out.at[:, pl.ds(pl.multiple_of((device * heads + h) * wide + t * HD, HD), HD)]
 
     def give(h, t):
         for k in range(1, ways):
@@ -351,33 +381,45 @@
         copy.start()
         back_locals.append(copy)
 
-    def combine(h):
-        arrive(back_edge_copies(h))
+    def combine(h, part):
+        arrive(back_edge_copies(h, part))
+        columns = parts[part]
         for t in range(PAIR):
-            value = own_grads[h, rows(t), :]
+            value = own_grads[h, rows(t), columns]
             if t < TILES:
                 near, far, table, base = from_prev, from_next, 0, t
                 near_at, far_at = t, 0
             else:
                 near, far, table, base = from_next, from_prev, 1, t - TILES
                 near_at, far_at = NAMED + t - TILES, TILES
-            value += near[h, rows(near_at), :].astype(F32)
+            value += near[h, rows(near_at), columns].astype(F32)
             for s in range(NAMED):
-                term = far[h, rows(far_at + s), :].astype(F32)
+                term = far[h, rows(far_at + s), columns].astype(F32)
                 value += jnp.where(slots[table, s] == base, term, 0.0)
-            joined[h, rows(t), HD:] = value.astype(BF16)
-        give(h, 1)
+            joined[h, rows(t), parts[part + 1]] = value.astype(BF16)
+        give(h, part + 1)
 
     edges(0)
+    edges(1)
+    attend(0, functools.partial(edges, 2))
+    give(0, 0)
+    attend(1, functools.partial(edges, 3))
+    give(1, 0)
+    combine(0, 0)
+    combine(0, 1)
+    attend(2)
+    give(2, 0)
+    attend(3)
+    give(3, 0)
+    combine(1, 0)
+    combine(1, 1)
+    combine(2, 0)
+    combine(2, 1)
+    combine(3, 0)
+    combine(3, 1)
+
     for h in range(heads):
-        attend(h, functools.partial(edges, h + 1) if h + 1 < heads else lambda: None)
-        give(h, 0)
-        if h > 0:
-            combine(h - 1)
-    combine(heads - 1)
-
-    for h in range(heads):
-        for t in range(2):
+        for t in range(3):
             for k in range(1, ways):
                 source = (me + ways - k) % ways
                 remote(
@@ -385,7 +427,8 @@
                     back_recv.at[h, k, t], peer_id(source, sizes),
                 ).wait_recv()
         leave(edge_copies(h))
-        leave(back_edge_copies(h))
+        leave(back_edge_copies(h, 0))
+        leave(back_edge_copies(h, 1))
     for copy in back_locals:
         copy.wait()
     for copy in sends + back_sends:
@@ -415,6 +458,7 @@
             pltpu.VMEM((ALL, BLK, 2 * HD), BF16),
             pltpu.VMEM((ALL * BLK, 2 * HD), F32),
             pltpu.VMEM((PAIR * LISTED + 1, BLK, 2 * HD), F32),
+            pltpu.VMEM((WIDTH * BLK, 2 * HD), F32), pltpu.VMEM((WIDTH * BLK, 2 * HD), F32),
             pltpu.VMEM((heads, full, 2 * HD), F32),
             edge, edge, edge, edge,
             pltpu.VMEM((heads, full, 3 * HD), BF16),
@@ -422,8 +466,8 @@
             pltpu.SMEM((4, 8, 128), I32), pltpu.SMEM((8, 128), I32),
             pltpu.SMEM((PAIR, LISTED), I32), pltpu.SMEM((2, NAMED), I32),
             dma((heads, ways, 3)), dma((heads, ways, 3)), dma((heads, 3)),
-            dma((heads, 2, 2)), dma((heads, 2, 2)), dma((heads, 2)), dma((heads, 2)),
-            dma((heads, ways, 2)), dma((heads, ways, 2)), dma((heads, 2)),
+            dma((heads, 2, 2)), dma((heads, 2, 2)), dma((heads, 2, 2)), dma((heads, 2, 2)),
+            dma((heads, ways, 3)), dma((heads, ways, 3)), dma((heads, 3)),
             dma((3,)), dma((3,)), dma((2,)),
         ],
         compiler_params=pltpu.CompilerParams(

time: 106 us -> 93.2 us (0.88)
  Pallas kernels: 104 us -> 91.1 us
    pallas_call x1, Pallas kernels: 104 us -> 91.1 us  [shards(): pl.pallas_call(functools.partial(layer_kernel, sizes), in_specs=[smem, sm...]
where the time goes in v2:
time: 93.2 us; the launch traced here: 92.7 us
  Pallas kernels  91.1 us (98%)
  local copies, waits for them, and re-layouts  1.67 us (2%)
    pallas_call x1, Pallas kernels, shards(): pl.pallas_call(functools.partial(layer_kernel, sizes), in_specs=[smem, sm...  91.1 us

profile of v2, /device:TPU:0, one launch (start us, length us, event | category | flops | bytes accessed | tf_op | source)
XLA Modules:
  0.0 92.7 jit_solution(4210285807116016188)
XLA Ops:
  0.0 91.1 %layer.1 = bf16[128,12288]{1,0:T(8,128)(2,1)S(1)} custom-call(s32[4,4]{1,0:T(4,128)} %key_lists.1, s32[4]{0:T(128)} %live_counts.1, bf16[128,12288]{1,0:T(8,128)(2,1)} %qkv.1, bf16[128,4096]{1,0:T(8,128)(2,1)} %grads.1), custom_call_target="tpu_custom_call" | custom-call | tf_op jit(solution)/shard_map/layer/pallas_call | solution.py:450
  91.1 1.7 %copy.6 = bf16[128,12288]{1,0:T(8,128)(2,1)} copy(bf16[128,12288]{1,0:T(8,128)(2,1)S(1)} %layer.1) | data formatting | bytes 6291456

commit v3 on v2

--- a/solution.py
+++ b/solution.py
@@ -16,8 +16,6 @@
 EDGE = NAMED + TILES
 ALL = 2 * EDGE + PAIR
 WIDTH = 3 + LISTED
-AHEAD = 1
-MIDDLE = 4
 SCALE = HD ** (-0.5)
 RATE = SCALE * 1.4426950408889634
 MESH = pl.DeviceIdType.MESH
@@ -139,7 +137,7 @@
     sizes, key_lists, live_counts, qkv, grads, out,
     own, left, right, stage, pairs, acc, chain, even, odd, own_grads, left_grads, right_grads, from_next, from_prev, joined,
     lists, chains, tab, links, places, slots,
-    send, recv, local, edge_send, edge_recv, back_edge_send, back_edge_recv, back_send, back_recv, back_local,
+    send, recv, edge_send, edge_recv, back_edge_send, back_edge_recv, back_send, back_recv,
     list_send, list_recv, table_sem,
 ):
     pairs_total, _, ways = sizes
@@ -154,12 +152,11 @@
 
     def piece(h, device, block, t):
         at = device * heads + h
-        start = pl.multiple_of(at * wide, HD)
-        if t == 0:
-            return qkv.at[:, pl.ds(start + HD, 2 * HD)], own.at[h, rows(block), kv]
-        if t == 1:
-            return qkv.at[:, pl.ds(start, HD)], own.at[h, rows(block), pl.ds(0, HD)]
-        return grads.at[:, pl.ds(pl.multiple_of(at * slim, HD), slim)], own.at[h, rows(block), pl.ds(wide, slim)]
+        if t == 3:
+            return grads.at[:, pl.ds(pl.multiple_of(at * slim, HD), slim)], own.at[h, rows(block), pl.ds(wide, slim)]
+        column = (t + 1) % 3 * HD
+        start = pl.multiple_of(at * wide + column, HD)
+        return qkv.at[:, pl.ds(start, HD)], own.at[h, rows(block), pl.ds(column, HD)]
 
     side = z - 1 + 2 * x
     beyond = (side >= 0) & (side < pairs_total)
@@ -171,34 +168,35 @@
     list_other.start()
     pl.when(beyond)(lambda: [c.start() for c in list_side] and None)
 
-    sends = []
-
     def fetch(h, kinds):
-        for k in range(1, ways):
-            peer = (me + k) % ways
-            for t in kinds:
+        for t in kinds:
+            for k in range(1, ways):
+                peer = (me + k) % ways
                 src, dst = piece(h, peer, me, t)
-                copy = remote(src, dst, send.at[h, k, t], recv.at[h, k, t], peer_id(peer, sizes))
-                copy.start()
-                sends.append(copy)
-        for t in kinds:
+                remote(src, dst, send.at[h], recv.at[h, t], peer_id(peer, sizes)).start()
             src, dst = piece(h, me, me, t)
-            pltpu.make_async_copy(src, dst, local.at[h, t]).start()
+            pltpu.make_async_copy(src, dst, recv.at[h, t]).start()
+
+    def settled(ref, sem):
+        pltpu.make_async_copy(ref, ref, sem).wait()
 
     def arrived(h, kinds):
         for t in kinds:
-            for k in range(1, ways):
-                source = (me + ways - k) % ways
-                src, dst = piece(h, source, source, t)
-                remote(src, dst, send.at[h, k, t], recv.at[h, k, t], peer_id(source, sizes)).wait_recv()
-            src, dst = piece(h, me, me, t)
-            pltpu.make_async_copy(src, dst, local.at[h, t]).wait()
-
-    for h in range(heads + AHEAD):
-        if h < heads:
-            fetch(h, (0,))
-        if h >= AHEAD:
-            fetch(h - AHEAD, (1, 2))
+            column = 3 * HD if t == 3 else (t + 1) % 3 * HD
+            settled(own.at[h, :, pl.ds(column, HD)], recv.at[h, t])
+
+    fetch(0, (0,))
+    fetch(0, (1,))
+    fetch(1, (0,))
+    fetch(1, (1,))
+    fetch(0, (2, 3))
+    fetch(2, (0,))
+    fetch(2, (1,))
+    fetch(1, (2, 3))
+    fetch(3, (0,))
+    fetch(3, (1,))
+    fetch(2, (2, 3))
+    fetch(3, (2, 3))
 
     @pl.when(z == 0)
     def _():
@@ -225,17 +223,19 @@
     copy.start()
     copy.wait()
 
-    def edge_copies(h):
+    def edge_copies(h, t):
+        part = pl.ds(t * HD, HD)
+        column = pl.ds((t + 1) * HD, HD)
         up = [
-            remote(src, left.at[h, part], edge_send.at[h, 0, n], edge_recv.at[h, 0, n], {"cz": z + 1})
-            for n, (src, part) in enumerate(
-                ((stage.at[h, 0], rows(0, NAMED)), (own.at[h, rows(TILES, TILES), kv], rows(NAMED, TILES)))
+            remote(src, left.at[h, place, part], edge_send.at[h, 0], edge_recv.at[h, 0, t], {"cz": z + 1})
+            for n, (src, place) in enumerate(
+                ((stage.at[h, 0, :, part], rows(0, NAMED)), (own.at[h, rows(TILES, TILES), column], rows(NAMED, TILES)))
             )
         ]
         down = [
-            remote(src, right.at[h, part], edge_send.at[h, 1, n], edge_recv.at[h, 1, n], {"cz": z - 1})
-            for n, (src, part) in enumerate(
-                ((stage.at[h, 1], rows(TILES, NAMED)), (own.at[h, rows(0, TILES), kv], rows(0, TILES)))
+            remote(src, right.at[h, place, part], edge_send.at[h, 1], edge_recv.at[h, 1, t], {"cz": z - 1})
+            for n, (src, place) in enumerate(
+                ((stage.at[h, 1, :, part], rows(TILES, NAMED)), (own.at[h, rows(0, TILES), column], rows(0, TILES)))
             )
         ]
         return up, down
@@ -244,11 +244,11 @@
         part = pl.ds(t * HD, HD)
         up = remote(
             right_grads.at[h, :, part], from_prev.at[h, :, part],
-            back_edge_send.at[h, 0, t], back_edge_recv.at[h, 0, t], {"cz": z + 1},
+            back_edge_send.at[h, 0], back_edge_recv.at[h, 0, t], {"cz": z + 1},
         )
         down = remote(
             left_grads.at[h, :, part], from_next.at[h, :, part],
-            back_edge_send.at[h, 1, t], back_edge_recv.at[h, 1, t], {"cz": z - 1},
+            back_edge_send.at[h, 1], back_edge_recv.at[h, 1, t], {"cz": z - 1},
         )
         return [up], [down]
 
@@ -257,29 +257,30 @@
         pl.when(inner[1])(lambda: [c.start() for c in up] and None)
         pl.when(inner[0])(lambda: [c.start() for c in down] and None)
 
-    def arrive(copies):
-        up, down = copies
-        pl.when(inner[0])(lambda: [c.wait_recv() for c in up] and None)
-        pl.when(inner[1])(lambda: [c.wait_recv() for c in down] and None)
-
-    def leave(copies):
-        up, down = copies
-        pl.when(inner[1])(lambda: [c.wait_send() for c in up] and None)
-        pl.when(inner[0])(lambda: [c.wait_send() for c in down] and None)
-
-    def edges(h):
-        arrived(h, (0,))
+    def arrive(h, t, refs, sems):
+        part = pl.ds(t * HD, HD)
+        pl.when(inner[0])(lambda: settled(refs[0].at[h, :, part], sems.at[h, 0, t]))
+        pl.when(inner[1])(lambda: settled(refs[1].at[h, :, part], sems.at[h, 1, t]))
+
+    def leave(h, refs, sems):
+        pl.when(inner[1])(lambda: settled(refs[0].at[h], sems.at[h, 0]))
+        pl.when(inner[0])(lambda: settled(refs[1].at[h], sems.at[h, 1]))
+
+    def edges(h, t):
+        arrived(h, (t,))
+        columns = slice((t + 1) * HD, (t + 2) * HD)
         for s in range(NAMED):
             for side in range(2):
-                chosen = own[h, rows(side * TILES), HD : 3 * HD]
-                for t in range(1, TILES):
-                    chosen = jnp.where(slots[side, s] == t, own[h, rows(side * TILES + t), HD : 3 * HD], chosen)
-                stage[h, side, rows(s), :] = chosen
-        start(edge_copies(h))
-
-    def attend(h, middle=None):
-        arrived(h, (1, 2))
-        arrive(edge_copies(h))
+                chosen = own[h, rows(side * TILES), columns]
+                for n in range(1, TILES):
+                    chosen = jnp.where(slots[side, s] == n, own[h, rows(side * TILES + n), columns], chosen)
+                stage[h, side, rows(s), t * HD : (t + 1) * HD] = chosen
+        start(edge_copies(h, t))
+
+    def attend(h, plan=()):
+        arrived(h, (2, 3))
+        arrive(h, 0, (left, right), edge_recv)
+        arrive(h, 1, (left, right), edge_recv)
         pairs[:EDGE] = left[h].reshape(EDGE, BLK, 2 * HD)
         pairs[EDGE : EDGE + PAIR] = own[h, :, HD : 3 * HD].reshape(PAIR, BLK, 2 * HD)
         pairs[EDGE + PAIR :] = right[h].reshape(EDGE, BLK, 2 * HD)
@@ -330,6 +331,8 @@
 
         def step(n, carry):
             i = 2 * n
+            for when, task in plan:
+                pl.when(n == when)(task)
             issue(i + 1, odd)
             settle(i, even)
             issue((i + 2) % PAIR, even)
@@ -337,12 +340,7 @@
             return carry
 
         issue(0, even)
-        if middle is None:
-            lax.fori_loop(0, PAIR // 2, step, 0)
-        else:
-            lax.fori_loop(0, MIDDLE // 2, step, 0)
-            middle()
-            lax.fori_loop(MIDDLE // 2, PAIR // 2, step, 0)
+        lax.fori_loop(0, PAIR // 2, step, 0)
 
         def total(p):
             value = acc[rows(p), :] + chain[links[1, p]]
@@ -362,27 +360,28 @@
         start(back_edge_copies(h, 1))
         lax.fori_loop(0, PAIR, own_total, 0)
 
-    back_sends, back_locals = [], []
     parts = [slice(t * HD, (t + 1) * HD) for t in range(3)]
 
     def column(device, h, t):
         return out.at[:, pl.ds(pl.multiple_of((device * heads + h) * wide + t * HD, HD), HD)]
 
+    def give_copy(h, t, k):
+        peer = (me + k) % ways
+        return remote(
+            joined.at[h, rows(peer), parts[t]], column(me, h, t), back_send.at[h], back_recv.at[h],
+            peer_id(peer, sizes),
+        )
+
+    def give_local(h, t):
+        return pltpu.make_async_copy(joined.at[h, rows(me), parts[t]], column(me, h, t), back_recv.at[h])
+
     def give(h, t):
         for k in range(1, ways):
-            peer = (me + k) % ways
-            copy = remote(
-                joined.at[h, rows(peer), parts[t]], column(me, h, t), back_send.at[h, k, t], back_recv.at[h, k, t],
-                peer_id(peer, sizes),
-            )
-            copy.start()
-            back_sends.append(copy)
-        copy = pltpu.make_async_copy(joined.at[h, rows(me), parts[t]], column(me, h, t), back_local.at[h, t])
-        copy.start()
-        back_locals.append(copy)
+            give_copy(h, t, k).start()
+        give_local(h, t).start()
 
     def combine(h, part):
-        arrive(back_edge_copies(h, part))
+        arrive(h, part, (from_prev, from_next), back_edge_recv)
         columns = parts[part]
         for t in range(PAIR):
             value = own_grads[h, rows(t), columns]
@@ -399,11 +398,13 @@
             joined[h, rows(t), parts[part + 1]] = value.astype(BF16)
         give(h, part + 1)
 
-    edges(0)
-    edges(1)
-    attend(0, functools.partial(edges, 2))
+    edges(0, 0)
+    edges(0, 1)
+    edges(1, 0)
+    edges(1, 1)
+    attend(0, [(2, functools.partial(edges, 2, 0)), (2, functools.partial(edges, 2, 1))])
     give(0, 0)
-    attend(1, functools.partial(edges, 3))
+    attend(1, [(2, functools.partial(edges, 3, 0)), (2, functools.partial(edges, 3, 1))])
     give(1, 0)
     combine(0, 0)
     combine(0, 1)
@@ -419,20 +420,11 @@
     combine(3, 1)
 
     for h in range(heads):
-        for t in range(3):
-            for k in range(1, ways):
-                source = (me + ways - k) % ways
-                remote(
-                    joined.at[h, rows(source), parts[t]], column(source, h, t), back_send.at[h, k, t],
-                    back_recv.at[h, k, t], peer_id(source, sizes),
-                ).wait_recv()
-        leave(edge_copies(h))
-        leave(back_edge_copies(h, 0))
-        leave(back_edge_copies(h, 1))
-    for copy in back_locals:
-        copy.wait()
-    for copy in sends + back_sends:
-        copy.wait_send()
+        settled(own.at[h, pl.ds(0, (ways - 1) * BLK)], send.at[h])
+        leave(h, (left, right), edge_send)
+        leave(h, (right_grads, left_grads), back_edge_send)
+        settled(joined.at[h, pl.ds(0, (ways - 1) * BLK)], back_send.at[h])
+        settled(out.at[:, pl.ds(0, ways * wide)], back_recv.at[h])
     list_other.wait_send()
     pl.when(beyond)(lambda: [c.wait_send() for c in list_side] and None)
 
@@ -465,9 +457,9 @@
             pltpu.VMEM((4, 8, 128), I32), pltpu.VMEM((8, 128), I32),
             pltpu.SMEM((4, 8, 128), I32), pltpu.SMEM((8, 128), I32),
             pltpu.SMEM((PAIR, LISTED), I32), pltpu.SMEM((2, NAMED), I32),
-            dma((heads, ways, 3)), dma((heads, ways, 3)), dma((heads, 3)),
-            dma((heads, 2, 2)), dma((heads, 2, 2)), dma((heads, 2, 2)), dma((heads, 2, 2)),
-            dma((heads, ways, 3)), dma((heads, ways, 3)), dma((heads, 3)),
+            dma((heads,)), dma((heads, 4)),
+            dma((heads, 2)), dma((heads, 2, 2)), dma((heads, 2)), dma((heads, 2, 2)),
+            dma((heads,)), dma((heads,)),
             dma((3,)), dma((3,)), dma((2,)),
         ],
         compiler_params=pltpu.CompilerParams(

time: 93.2 us -> 87.6 us (0.940)
  Pallas kernels: 91.1 us -> 85.7 us
    pallas_call x1, Pallas kernels: 91.1 us -> 85.7 us  [shards(): pl.pallas_call(functools.partial(layer_kernel, sizes), in_specs=[smem, sm...]
where the time goes in v3:
time: 87.6 us; the launch traced here: 87.4 us
  Pallas kernels  85.7 us (98%)
  local copies, waits for them, and re-layouts  1.67 us (2%)
    pallas_call x1, Pallas kernels, shards(): pl.pallas_call(functools.partial(layer_kernel, sizes), in_specs=[smem, sm...  85.7 us

profile of v3, /device:TPU:0, one launch (start us, length us, event | category | flops | bytes accessed | tf_op | source)
XLA Modules:
  0.0 87.4 jit_solution(12492608313788954687)
XLA Ops:
  0.0 85.7 %layer.1 = bf16[128,12288]{1,0:T(8,128)(2,1)S(1)} custom-call(s32[4,4]{1,0:T(4,128)} %key_lists.1, s32[4]{0:T(128)} %live_counts.1, bf16[128,12288]{1,0:T(8,128)(2,1)} %qkv.1, bf16[128,4096]{1,0:T(8,128)(2,1)} %grads.1), custom_call_target="tpu_custom_call" | custom-call | tf_op jit(solution)/shard_map/layer/pallas_call | solution.py:442
  85.7 1.7 %copy.6 = bf16[128,12288]{1,0:T(8,128)(2,1)} copy(bf16[128,12288]{1,0:T(8,128)(2,1)S(1)} %layer.1) | data formatting | bytes 6291456

commit v4 on v3

--- a/solution.py
+++ b/solution.py
@@ -136,7 +136,7 @@
 def layer_kernel(
     sizes, key_lists, live_counts, qkv, grads, out,
     own, left, right, stage, pairs, acc, chain, even, odd, own_grads, left_grads, right_grads, from_next, from_prev, joined,
-    lists, chains, tab, links, places, slots,
+    lists, chains, tab, links, places, slots, named_here, live_here,
     send, recv, edge_send, edge_recv, back_edge_send, back_edge_recv, back_send, back_recv,
     list_send, list_recv, table_sem,
 ):
@@ -147,7 +147,10 @@
     wide, slim = 3 * HD, HD
     inner = (z > 0, z < pairs_total - 1)
     kv = pl.ds(HD, 2 * HD)
-    pack(lists, key_lists, live_counts, pairs_total, z, x)
+    own_lists = pltpu.make_async_copy(key_lists, named_here, table_sem.at[0])
+    own_counts = pltpu.make_async_copy(live_counts, live_here, table_sem.at[1])
+    own_lists.start()
+    own_counts.start()
     greet(sizes)
 
     def piece(h, device, block, t):
@@ -165,9 +168,6 @@
         remote(lists.at[x], lists.at[2 + x], list_send.at[1], list_recv.at[1 + x], {"cz": side}),
         remote(lists.at[x], lists.at[2 + x], list_send.at[2], list_recv.at[1 + x], {"cz": side, "cx": 1 - x}),
     ]
-    list_other.start()
-    pl.when(beyond)(lambda: [c.start() for c in list_side] and None)
-
     def fetch(h, kinds):
         for t in kinds:
             for k in range(1, ways):
@@ -177,6 +177,12 @@
             src, dst = piece(h, me, me, t)
             pltpu.make_async_copy(src, dst, recv.at[h, t]).start()
 
+    own_lists.wait()
+    own_counts.wait()
+    pack(lists, named_here, live_here, pairs_total, z, x)
+    list_other.start()
+    pl.when(beyond)(lambda: [c.start() for c in list_side] and None)
+
     def settled(ref, sem):
         pltpu.make_async_copy(ref, ref, sem).wait()
 
@@ -187,6 +193,7 @@
 
     fetch(0, (0,))
     fetch(0, (1,))
+
     fetch(1, (0,))
     fetch(1, (1,))
     fetch(0, (2, 3))
@@ -435,13 +442,12 @@
     sizes = (lax.axis_size("cz"), heads_total, ways)
     heads = qkv.shape[1] // (3 * HD) // ways
     full = qkv.shape[0] * ways
-    smem = pl.BlockSpec(memory_space=pltpu.SMEM)
     hbm = pl.BlockSpec(memory_space=pltpu.HBM)
     dma = pltpu.SemaphoreType.DMA
     edge = pltpu.VMEM((heads, EDGE * BLK, 2 * HD), BF16)
     return pl.pallas_call(
         functools.partial(layer_kernel, sizes),
-        in_specs=[smem, smem, hbm, hbm],
+        in_specs=[hbm] * 4,
         out_specs=pl.BlockSpec(memory_space=pltpu.VMEM),
         out_shape=pltpu.VMEM(qkv.shape, BF16),
         scratch_shapes=[
@@ -457,6 +463,7 @@
             pltpu.VMEM((4, 8, 128), I32), pltpu.VMEM((8, 128), I32),
             pltpu.SMEM((4, 8, 128), I32), pltpu.SMEM((8, 128), I32),
             pltpu.SMEM((PAIR, LISTED), I32), pltpu.SMEM((2, NAMED), I32),
+            pltpu.SMEM((TILES, LISTED), I32), pltpu.SMEM((TILES,), I32),
             dma((heads,)), dma((heads, 4)),
             dma((heads, 2)), dma((heads, 2, 2)), dma((heads, 2)), dma((heads, 2, 2)),
             dma((heads,)), dma((heads,)),

time: 87.6 us -> 86.7 us (0.990)
  Pallas kernels: 85.7 us -> 84.8 us
    pallas_call x1, Pallas kernels: 85.7 us -> 84.8 us  [shards(): pl.pallas_call(functools.partial(layer_kernel, sizes), in_specs=[hbm] * 4...]
where the time goes in v4:
time: 86.7 us; the launch traced here: 86.5 us
  Pallas kernels  84.8 us (98%)
  local copies, waits for them, and re-layouts  1.67 us (2%)
    pallas_call x1, Pallas kernels, shards(): pl.pallas_call(functools.partial(layer_kernel, sizes), in_specs=[hbm] * 4...  84.8 us

profile of v4, /device:TPU:0, one launch (start us, length us, event | category | flops | bytes accessed | tf_op | source)
XLA Modules:
  0.0 86.5 jit_solution(13828556023056685142)
XLA Ops:
  0.0 84.8 %layer.1 = bf16[128,12288]{1,0:T(8,128)(2,1)S(1)} custom-call(s32[4,4]{1,0:T(4,128)} %key_lists.1, s32[4]{0:T(128)} %live_counts.1, bf16[128,12288]{1,0:T(8,128)(2,1)} %qkv.1, bf16[128,4096]{1,0:T(8,128)(2,1)} %grads.1), custom_call_target="tpu_custom_call" | custom-call | tf_op jit(solution)/shard_map/layer/pallas_call | solution.py:448
  84.8 1.7 %copy.6 = bf16[128,12288]{1,0:T(8,128)(2,1)} copy(bf16[128,12288]{1,0:T(8,128)(2,1)S(1)} %layer.1) | data formatting | bytes 6291456

commit v5 on v4

--- a/solution.py
+++ b/solution.py
@@ -317,9 +317,9 @@
             tiles = [products[n * BLK : (n + 1) * BLK, :HD] for n in range(WIDTH)]
             peaks = [jnp.max(s.reshape(BLK // 8, 8, HD), axis=0) for s in tiles]
             peaks = [s if ok is None else jnp.where(ok, s, -1e30) for s, ok in zip(peaks, usable)]
-            shift = jnp.max(functools.reduce(jnp.maximum, peaks), axis=0, keepdims=True) * -RATE
-            shifts = [shift if ok is None else jnp.where(ok, shift, -1e30) for ok in usable]
-            powers = jnp.concatenate([jnp.exp2(s * RATE + b) for s, b in zip(tiles, shifts)], axis=0)
+            top = jnp.max(functools.reduce(jnp.maximum, peaks), axis=0, keepdims=True)
+            tops = [top if ok is None else jnp.where(ok, top, 1e30) for ok in usable]
+            powers = jnp.concatenate([jnp.exp2((s - b) * RATE) for s, b in zip(tiles, tops)], axis=0)
             dp = products[:, HD:]
             over = 1.0 / jnp.sum(powers, axis=0, keepdims=True)
             soft = powers * over

time: 86.7 us -> 86.7 us (level)
  no operation moved by 1% of the time
where the time goes in v5:
time: 86.7 us; the launch traced here: 86.5 us
  Pallas kernels  84.8 us (98%)
  local copies, waits for them, and re-layouts  1.67 us (2%)
    pallas_call x1, Pallas kernels, shards(): pl.pallas_call(functools.partial(layer_kernel, sizes), in_specs=[hbm] * 4...  84.8 us

profile of v5, /device:TPU:0, one launch (start us, length us, event | category | flops | bytes accessed | tf_op | source)
XLA Modules:
  0.0 86.5 jit_solution(1028272166397986325)
XLA Ops:
  0.0 84.8 %layer.1 = bf16[128,12288]{1,0:T(8,128)(2,1)S(1)} custom-call(s32[4,4]{1,0:T(4,128)} %key_lists.1, s32[4]{0:T(128)} %live_counts.1, bf16[128,12288]{1,0:T(8,128)(2,1)} %qkv.1, bf16[128,4096]{1,0:T(8,128)(2,1)} %grads.1), custom_call_target="tpu_custom_call" | custom-call | tf_op jit(solution)/shard_map/layer/pallas_call | solution.py:448
  84.8 1.7 %copy.6 = bf16[128,12288]{1,0:T(8,128)(2,1)} copy(bf16[128,12288]{1,0:T(8,128)(2,1)S(1)} %layer.1) | data formatting | bytes 6291456

commit v6 on v5

--- a/solution.py
+++ b/solution.py
@@ -11,6 +11,7 @@
 BLK = 128
 TILES = 4
 LISTED = 4
+CUTS = 2
 NAMED = 2
 PAIR = 2 * TILES
 EDGE = NAMED + TILES
@@ -170,10 +171,12 @@
     ]
     def fetch(h, kinds):
         for t in kinds:
-            for k in range(1, ways):
-                peer = (me + k) % ways
-                src, dst = piece(h, peer, me, t)
-                remote(src, dst, send.at[h], recv.at[h, t], peer_id(peer, sizes)).start()
+            for part in range(CUTS):
+                few = pl.ds(part * (BLK // CUTS), BLK // CUTS)
+                for k in range(1, ways):
+                    peer = (me + k) % ways
+                    src, dst = piece(h, peer, me, t)
+                    remote(src.at[few], dst.at[few], send.at[h], recv.at[h, t], peer_id(peer, sizes)).start()
             src, dst = piece(h, me, me, t)
             pltpu.make_async_copy(src, dst, recv.at[h, t]).start()
 

time: 86.7 us -> 86.5 us (level)
  no operation moved by 1% of the time
where the time goes in v6:
time: 86.5 us; the launch traced here: 86.3 us
  Pallas kernels  84.6 us (98%)
  local copies, waits for them, and re-layouts  1.67 us (2%)
    pallas_call x1, Pallas kernels, shards(): pl.pallas_call(functools.partial(layer_kernel, sizes), in_specs=[hbm] * 4...  84.6 us

profile of v6, /device:TPU:0, one launch (start us, length us, event | category | flops | bytes accessed | tf_op | source)
XLA Modules:
  0.0 86.3 jit_solution(13399850623622032541)
XLA Ops:
  0.0 84.6 %layer.1 = bf16[128,12288]{1,0:T(8,128)(2,1)S(1)} custom-call(s32[4,4]{1,0:T(4,128)} %key_lists.1, s32[4]{0:T(128)} %live_counts.1, bf16[128,12288]{1,0:T(8,128)(2,1)} %qkv.1, bf16[128,4096]{1,0:T(8,128)(2,1)} %grads.1), custom_call_target="tpu_custom_call" | custom-call | tf_op jit(solution)/shard_map/layer/pallas_call | solution.py:451
  84.6 1.7 %copy.6 = bf16[128,12288]{1,0:T(8,128)(2,1)} copy(bf16[128,12288]{1,0:T(8,128)(2,1)S(1)} %layer.1) | data formatting | bytes 6291456
